TPU v7x, 512 devices: a whole 4x4x16 slice. The times are simulated.
512 devices in a mesh: dp: 16 (over x, y_hi, core), ctx: 32 (over y_lo, z).
Axes of the slice: x: 4, y: 4 (y_hi: 2, y_lo: 2; y = y_hi * 2 + y_lo), z: 16, core: 2. Of those that a mesh axis runs over, the one named last changes fastest.
Arguments:
- queries: bfloat16 [16, 4096, 2048], P('dp', 'ctx'), may hold values from -6 to 6
- keys: bfloat16 [16, 4096, 2048], P('dp', 'ctx'), may hold values from -6 to 6
- values: bfloat16 [16, 4096, 2048], P('dp', 'ctx'), may hold values from -6 to 6
- out_grad: bfloat16 [16, 4096, 2048], P('dp', 'ctx'), may hold values from -6 to 6
- out_proj: bfloat16 [2048, 2048], P('dp'), may hold values from -0.125 to 0.125
- attn_out: bfloat16 [16, 4096, 2048], P('dp', 'ctx'), may hold values from -3 to 3
- log_sum: float32 [16, 16, 4096], P('dp', None, 'ctx'), may hold values from 3 to 5
- group_order: int32 [16, 128], P('dp'), may hold values from 0 to 127, each once within a row
Outputs:
- query_grad: bfloat16 [16, 4096, 2048], P('dp', 'ctx')
- key_grad: bfloat16 [16, 4096, 2048], P('dp', 'ctx')
- value_grad: bfloat16 [16, 4096, 2048], P('dp', 'ctx')
Inputs may be any that keep to these rules, and one draw needn't show every extreme that they name: `group_order`: each row holds every number once.
All inputs are finite; a program needn't handle non-finite values.
Results may differ from a plain program's by a relative error of at most 0.0075.
Values may be sent and summed in bfloat16 or wider, within the bound.
A program may use at most 64 MiB of HBM per device.

v0:
```python
import jax
import jax.numpy as jnp
from jax import lax
from jax.sharding import PartitionSpec as P

GROUP = 32


def shifted(array, axis, by):
    size = lax.axis_size(axis)
    return lax.ppermute(array, axis, [(i, (i + by) % size) for i in range(size)])


def pair_grads(query_blk, grad_blk, lse_blk, delta_blk, query_pos, key_blk, value_blk, key_pos):
    factor = query_blk.shape[2] ** (-0.5)
    scores = (
        jnp.einsum("qhd,khd->hqk", query_blk, key_blk, preferred_element_type=jnp.float32) * factor
    )
    visible = key_pos[None, None, :] <= query_pos[None, :, None]
    probs = jnp.where(visible, jnp.exp(scores - lse_blk[:, :, None]), 0.0)
    probs_low = probs.astype(jnp.bfloat16)
    value_part = jnp.einsum("hqk,qhd->khd", probs_low, grad_blk, preferred_element_type=jnp.float32)
    dprobs = jnp.einsum("qhd,khd->hqk", grad_blk, value_blk, preferred_element_type=jnp.float32)
    dscores = (probs * (dprobs - delta_blk[:, :, None])).astype(jnp.bfloat16)
    query_part = (
        jnp.einsum("hqk,khd->qhd", dscores, key_blk, preferred_element_type=jnp.float32) * factor
    )
    key_part = (
        jnp.einsum("hqk,qhd->khd", dscores, query_blk, preferred_element_type=jnp.float32) * factor
    )
    rows = query_blk.shape[0]
    width = query_blk.shape[1] * query_blk.shape[2]
    return (
        query_part.reshape(rows, width),
        key_part.reshape(key_blk.shape[0], width),
        value_part.reshape(key_blk.shape[0], width),
    )


def on_device(queries, keys, values, out_grad, out_proj, attn_out, log_sum, group_order):
    tokens = queries.shape[1]
    width = queries.shape[2]
    heads = log_sum.shape[1]
    head_size = width // heads
    upstream = out_grad[0]
    attn_full = jnp.dot(
        upstream,
        lax.all_gather(out_proj, "dp", axis=0, tiled=True),
        preferred_element_type=jnp.float32,
    )
    attn_grad = attn_full.astype(jnp.bfloat16)
    grad_blk = attn_grad.reshape(tokens, heads, head_size)
    out_blk = attn_out[0].reshape(tokens, heads, head_size)
    delta = jnp.sum(grad_blk.astype(jnp.float32) * out_blk.astype(jnp.float32), axis=2).T
    lse_own = log_sum[0]
    order = group_order[0]
    per_block = tokens // GROUP
    cycle_size = lax.axis_size("ctx")
    here = lax.axis_index("ctx")

    def positions(device):
        group_ids = lax.dynamic_slice_in_dim(order, device * per_block, per_block)
        offsets = jnp.arange(GROUP, dtype=jnp.int32)
        return (group_ids[:, None] * GROUP + offsets[None, :]).reshape(tokens)

    own_pos = positions(here)
    query_blk = queries[0].reshape(tokens, heads, head_size)
    key_flat = keys[0]
    value_flat = values[0]
    key_blk = key_flat.reshape(tokens, heads, head_size)
    value_blk = value_flat.reshape(tokens, heads, head_size)
    own = pair_grads(query_blk, grad_blk, lse_own, delta, own_pos, key_blk, value_blk, own_pos)
    key_prev, value_prev = shifted((key_flat, value_flat), "ctx", 1)
    prev_pos = positions((here - 1 + cycle_size) % cycle_size)
    cross = pair_grads(
        query_blk,
        grad_blk,
        lse_own,
        delta,
        own_pos,
        key_prev.reshape(tokens, heads, head_size),
        value_prev.reshape(tokens, heads, head_size),
        prev_pos,
    )
    key_back, value_back = shifted((cross[1], cross[2]), "ctx", -1)
    query_total = own[0] + cross[0]
    key_total = own[1] + key_back
    value_total = own[2] + value_back
    return (
        query_total.astype(jnp.bfloat16).reshape(1, tokens, width),
        key_total.astype(jnp.bfloat16).reshape(1, tokens, width),
        value_total.astype(jnp.bfloat16).reshape(1, tokens, width),
    )


def solution(mesh):
    return jax.shard_map(
        on_device,
        mesh=mesh,
        in_specs=(
            P("dp", "ctx", None),
            P("dp", "ctx", None),
            P("dp", "ctx", None),
            P("dp", "ctx", None),
            P("dp", None),
            P("dp", "ctx", None),
            P("dp", None, "ctx"),
            P("dp", None),
        ),
        out_specs=(P("dp", "ctx", None), P("dp", "ctx", None), P("dp", "ctx", None)),
        check_vma=False,
    )
```

profile of v0, /device:TPU:1, one launch (start us, length us, event | category | flops | bytes accessed | tf_op | source)
XLA Modules:
  0.0 186.6 jit_solution(16854233429764616080)
XLA Ops:
  7.2 0.0 copy-start
  7.2 0.0 all-gather.2.cloned.1.call-start
  7.2 0.7 all-gather.2.cloned.1.call-update
  7.9 2.0 %copy.64 = bf16[1,128,2048]{1,2,0:T(8,128)(2,1)} copy(bf16[1,128,2048]{2,1,0:T(8,128)(2,1)} %param.10) | data formatting | bytes 1048576 | tf_op args[2]
  10.0 4.4 %collective-permute-start.1 = (bf16[128,2048]{0,1:T(8,128)(2,1)}, bf16[128,2048]{0,1:T(8,128)(2,1)}, u32[]{:S(2)}, u32[]{:S(2)}) collective-permute-start(bf16[128,2048]{0,1:T(8,128)(2,1)} %bitcast.7), channel_id=1, source_target_pairs={{0,1},{1,2},{2,3},{3,4},{4,5},{5,6},{6,7},{7,8},{8,9},{9,10},{10,1... | collective-permute-start | bytes 1572872 | tf_op jit(solution)/shard_map/ppermute | solution.py:11
  14.3 1.3 copy.89
  15.6 0.0 copy-start.2
  15.7 3.5 %collective-permute-start = (bf16[128,2048]{0,1:T(8,128)(2,1)S(1)}, bf16[128,2048]{0,1:T(8,128)(2,1)S(1)}, u32[]{:S(2)}, u32[]{:S(2)}) collective-permute-start(bf16[128,2048]{0,1:T(8,128)(2,1)S(1)} %bitcast.70), channel_id=1, source_target_pairs={{0,1},{1,2},{2,3},{3,4},{4,5},{5,6},{6,7},{7,8},{8,9},{9,10},{10,1... | collective-permute-start | bytes 1572872 | tf_op jit(solution)/shard_map/ppermute | solution.py:11
  19.2 0.8 multiply_bitcast_fusion
  20.0 1.1 convert_bitcast_fusion
  21.2 0.1 iota_add_fusion
  21.3 0.1 add.89
  21.3 0.1 add.82
  21.4 1.3 copy.88
  22.7 2.0 %copy.91 = bf16[16,8,16,128]{3,2,1,0:T(8,128)(2,1)} copy(bf16[16,8,16,128]{3,1,2,0:T(8,128)(2,1)} %bitcast.78) | data formatting | bytes 1048576
  24.7 1.3 copy.92
  26.0 0.1 broadcast_compare_fusion
  26.1 0.5 fusion.10
  26.6 19.5 %collective-permute-done = bf16[128,2048]{0,1:T(8,128)(2,1)S(1)} collective-permute-done((bf16[128,2048]{0,1:T(8,128)(2,1)S(1)}, bf16[128,2048]{0,1:T(8,128)(2,1)S(1)}, u32[]{:S(2)}, u32[]{:S(2)}) %collective-permute-start) | collective-permute-done | bytes 524320 | tf_op jit(solution)/shard_map/ppermute | solution.py:11
  46.1 1.5 fusion.6
  47.6 57.5 %all-gather.2.cloned.1.call-done = bf16[2048,2048]{1,0:T(8,128)(2,1)} async-done(((bf16[128,2048]{1,0:T(8,128)(2,1)}), bf16[2048,2048]{1,0:T(8,128)(2,1)}) %all-gather.2.cloned.1.call-update) | async-done | bytes 8388624 | tf_op jit(solution)/shard_map/all_gather | solution.py:48
  105.2 4.6 %fusion.15 = bf16[16,8,16,128]{3,1,2,0:T(8,128)(2,1)S(1)} fusion(bf16[2048,2048]{1,0:T(8,128)(2,1)} %all-gather.2.cloned.1.call-done, bf16[1,128,2048]{2,1,0:T(8,128)(2,1)S(1)} %copy-done), kind=kOutput, calls=%fused_computation.23 | convolution fusion | flops 1074003968 | bytes 9437184 | tf_op jit(solution)/shard_map/dot_general | solution.py:46
  109.8 0.1 copy.90
  109.9 0.5 copy.76
  110.4 1.3 fusion.22
  111.7 2.5 %copy.79 = f32[128,2048]{1,0:T(8,128)} copy(f32[128,2048]{0,1:T(8,128)} %bitcast.74) | data formatting | bytes 2097152 | tf_op jit(solution)/shard_map/reshape | solution.py:36
  114.2 2.5 %fusion.20 = f32[16,128,128]{2,1,0:T(8,128)} fusion(bf16[128,16,128]{0,2,1:T(8,128)(2,1)S(1)} %copy.76, f32[16,128,128]{2,1,0:T(8,128)} %fusion.6), kind=kOutput, calls=%fused_computation.32 | convolution fusion | flops 67371008 | bytes 2621440 | tf_op jit(solution)/shard_map/hqk,qhd->khd/dot_general | solution.py:22
  116.7 2.6 %copy.78 = f32[128,2048]{1,0:T(8,128)} copy(f32[128,2048]{0,1:T(8,128)} %bitcast.75) | data formatting | bytes 2097152 | tf_op jit(solution)/shard_map/reshape | solution.py:36
  119.3 1.6 multiply_reduce_fusion
  120.9 0.1 copy.59
  120.9 1.9 %fusion.12 = bf16[16,128,128]{2,1,0:T(8,128)(2,1)S(1)} fusion(f32[16,128,128]{2,1,0:T(8,128)} %fusion.6, bf16[128,16,128]{0,2,1:T(8,128)(2,1)S(1)} %copy.76, bf16[128,16,128]{0,2,1:T(8,128)(2,1)} %bitcast.8, f32[16,128]{1,0:T(8,128)S(1)} %copy.59), kind=kOutput, calls=%fused_computation.20 | convolution fusion | flops 67895296 | bytes 2629632 | tf_op jit(solution)/shard_map/qhd,khd->hqk/dot_general | solution.py:23
  122.9 1.5 fusion
  124.4 2.6 %copy.75 = f32[128,16,128]{0,2,1:T(8,128)} copy(f32[128,16,128]{2,0,1:T(8,128)} %fusion) | data formatting | bytes 2097152 | tf_op jit(solution)/shard_map/mul | solution.py:29
  126.9 5.7 %collective-permute-start.2 = (f32[128,2048]{0,1:T(8,128)}, f32[128,2048]{0,1:T(8,128)}, u32[]{:S(2)}, u32[]{:S(2)}) collective-permute-start(f32[128,2048]{0,1:T(8,128)} %bitcast.82), channel_id=1, source_target_pairs={{0,31},{1,0},{2,1},{3,2},{4,3},{5,4},{6,5},{7,6},{8,7},{9,8},{10,9... | collective-permute-start | bytes 3145736 | tf_op jit(solution)/shard_map/ppermute | solution.py:11
  132.6 3.0 %collective-permute-start.3 = (f32[128,2048]{1,0:T(8,128)}, f32[128,2048]{1,0:T(8,128)}, u32[]{:S(2)}, u32[]{:S(2)}) collective-permute-start(f32[128,2048]{1,0:T(8,128)} %copy.78), channel_id=1, source_target_pairs={{0,31},{1,0},{2,1},{3,2},{4,3},{5,4},{6,5},{7,6},{8,7},{9,8},{10,9... | collective-permute-start | bytes 3145736 | tf_op jit(solution)/shard_map/ppermute | solution.py:11
  135.6 1.6 fusion.11
  137.3 0.8 copy-done.1
  138.1 1.6 fusion.24
  139.7 1.5 fusion.14
  141.2 0.3 copy.69
  141.5 1.0 copy.80
  142.5 2.6 %fusion.1 = f32[128,16,128]{2,0,1:T(8,128)} fusion(bf16[16,128,128]{2,1,0:T(8,128)(2,1)} %copy-done.1, bf16[128,16,128]{0,2,1:T(8,128)(2,1)S(1)} %bitcast.67), kind=kOutput, calls=%fused_computation.4 | convolution fusion | flops 67371008 | bytes 2097152 | tf_op jit(solution)/shard_map/hqk,qhd->khd/dot_general | solution.py:29
  145.1 1.6 copy.72
  146.6 8.5 %collective-permute-done.2 = f32[128,2048]{0,1:T(8,128)} collective-permute-done((f32[128,2048]{0,1:T(8,128)}, f32[128,2048]{0,1:T(8,128)}, u32[]{:S(2)}, u32[]{:S(2)}) %collective-permute-start.2) | collective-permute-done | bytes 1048608 | tf_op jit(solution)/shard_map/ppermute | solution.py:11
  155.2 1.3 fusion.16
  156.5 1.0 copy.81
  157.5 20.1 %collective-permute-done.3 = f32[128,2048]{1,0:T(8,128)} collective-permute-done((f32[128,2048]{1,0:T(8,128)}, f32[128,2048]{1,0:T(8,128)}, u32[]{:S(2)}, u32[]{:S(2)}) %collective-permute-start.3) | collective-permute-done | bytes 1048608 | tf_op jit(solution)/shard_map/ppermute | solution.py:11
  177.6 2.1 %fusion.17 = bf16[1,128,2048]{2,1,0:T(8,128)(2,1)} fusion(f32[128,2048]{1,0:T(8,128)S(1)} %copy-done.3, f32[128,2048]{1,0:T(8,128)} %collective-permute-done.3), kind=kLoop, calls=%fused_computation.29 | loop fusion | flops 524288 | bytes 2621440 | tf_op jit(solution)/shard_map/reshape | solution.py:92
  (10 shorter events, 0.0 us)
Async XLA Ops:
  7.2 98.0 %copy-start = (bf16[1,128,2048]{2,1,0:T(8,128)(2,1)S(1)}, bf16[1,128,2048]{2,1,0:T(8,128)(2,1)}, u32[]{:S(2)}) copy-start(bf16[1,128,2048]{2,1,0:T(8,128)(2,1)} %param.11) | copy-start | bytes 1572868
  7.2 18.9 %copy-start.5 = (f32[1,16,128]{2,1,0:T(8,128)S(1)}, f32[1,16,128]{2,1,0:T(8,128)}, u32[]{:S(2)}) copy-start(f32[1,16,128]{2,1,0:T(8,128)} %param.14) | copy-start | bytes 24580
  7.2 98.0 %all-gather.2.cloned.1.call-start = ((), (), s32[]{:S(2)}) async-start(), calls=%async_computation | async-start | bytes 8912896 | tf_op jit(solution)/shard_map/all_gather | solution.py:48
  10.0 111.0 %collective-permute-start.1 = (bf16[128,2048]{0,1:T(8,128)(2,1)}, bf16[128,2048]{0,1:T(8,128)(2,1)}, u32[]{:S(2)}, u32[]{:S(2)}) collective-permute-start(bf16[128,2048]{0,1:T(8,128)(2,1)} %bitcast.7), channel_id=1, source_target_pairs={{0,1},{1,2},{2,3},{3,4},{4,5},{5,6},{6,7},{7,8},{8,9},{9,10},{10,1... | collective-permute-start | bytes 1572872 | tf_op jit(solution)/shard_map/ppermute | solution.py:11
  15.6 94.2 %copy-start.2 = (bf16[1,128,2048]{1,2,0:T(8,128)(2,1)}, bf16[1,128,2048]{1,2,0:T(8,128)(2,1)S(1)}, u32[]{:S(2)}) copy-start(bf16[1,128,2048]{1,2,0:T(8,128)(2,1)S(1)} %copy.89) | copy-start | bytes 1572868
  15.7 30.5 %collective-permute-start = (bf16[128,2048]{0,1:T(8,128)(2,1)S(1)}, bf16[128,2048]{0,1:T(8,128)(2,1)S(1)}, u32[]{:S(2)}, u32[]{:S(2)}) collective-permute-start(bf16[128,2048]{0,1:T(8,128)(2,1)S(1)} %bitcast.70), channel_id=1, source_target_pairs={{0,1},{1,2},{2,3},{3,4},{4,5},{5,6},{6,7},{7,8},{8,9},{9,10},{10,1... | collective-permute-start | bytes 1572872 | tf_op jit(solution)/shard_map/ppermute | solution.py:11
  46.1 59.0 %copy-start.4 = (bf16[128,2048]{0,1:T(8,128)(2,1)}, bf16[128,2048]{0,1:T(8,128)(2,1)S(1)}, u32[]{:S(2)}) copy-start(bf16[128,2048]{0,1:T(8,128)(2,1)S(1)} %collective-permute-done) | copy-start | bytes 1572868
  126.9 28.2 %collective-permute-start.2 = (f32[128,2048]{0,1:T(8,128)}, f32[128,2048]{0,1:T(8,128)}, u32[]{:S(2)}, u32[]{:S(2)}) collective-permute-start(f32[128,2048]{0,1:T(8,128)} %bitcast.82), channel_id=1, source_target_pairs={{0,31},{1,0},{2,1},{3,2},{4,3},{5,4},{6,5},{7,6},{8,7},{9,8},{10,9... | collective-permute-start | bytes 3145736 | tf_op jit(solution)/shard_map/ppermute | solution.py:11
  132.6 45.0 %collective-permute-start.3 = (f32[128,2048]{1,0:T(8,128)}, f32[128,2048]{1,0:T(8,128)}, u32[]{:S(2)}, u32[]{:S(2)}) collective-permute-start(f32[128,2048]{1,0:T(8,128)} %copy.78), channel_id=1, source_target_pairs={{0,31},{1,0},{2,1},{3,2},{4,3},{5,4},{6,5},{7,6},{8,7},{9,8},{10,9... | collective-permute-start | bytes 3145736 | tf_op jit(solution)/shard_map/ppermute | solution.py:11
  137.3 0.8 copy-start.1
  138.1 39.6 %copy-start.3 = (f32[128,2048]{1,0:T(8,128)S(1)}, f32[128,2048]{1,0:T(8,128)}, u32[]{:S(2)}) copy-start(f32[128,2048]{1,0:T(8,128)} %copy.79) | copy-start | bytes 3145732
Sparse Core Ops, SparseCore 0:
  11.3 93.8 all-gather.1
where the time goes:
time: 188 us; the launch traced here: 187 us
  waiting for transfers between devices  106 us (56%)
  matrix products  21.2 us (11%)
  local copies, waits for them, and re-layouts  21 us (11%)
  starting transfers between devices  16.6 us (9%)
  between operations  14.2 us (8%)
  other arithmetic  7.12 us (4%)
    all_gather x1, waiting for transfers between devices, on_device(): lax.all_gather(out_proj, 'dp', axis=0, tiled=True)  57.5 us
    ppermute x4, waiting for transfers between devices, shifted(): lax.ppermute(array, axis, [(i, (i + by) % size) for i in range(size)])  48.2 us
    ppermute x4, starting transfers between devices, shifted(): lax.ppermute(array, axis, [(i, (i + by) % size) for i in range(size)])  16.6 us
    unnamed x18, local copies, waits for them, and re-layouts  8.2 us
    reshape x2, local copies, waits for them, and re-layouts, pair_grads(): value_part.reshape(key_blk.shape[0], width)  5.09 us
    dot_general x1, matrix products, on_device(): jnp.dot(upstream, lax.all_gather(out_proj, 'dp', axis=0, tiled=True), pre...  4.65 us
    mul x2, local copies, waits for them, and re-layouts, pair_grads(): jnp.einsum('hqk,qhd->khd', dscores, query_blk, preferred_element_type=jnp...  4.11 us
    dot_general x2, matrix products, pair_grads(): jnp.einsum('hqk,qhd->khd', dscores, query_blk, preferred_element_type=jnp...  4.05 us
  transfers between devices with their start and end apart: 5, of which 4 were waited for; matrix products, arithmetic and copies ran while one was open for 22% of the time, Pallas kernels for 0%

commit v1 on v0

v1 whole, which is shorter than its diff:
```python
import functools

import jax
import jax.numpy as jnp
from jax import lax
from jax.experimental import pallas as pl
from jax.experimental.pallas import tpu as pltpu
from jax.sharding import PartitionSpec as P

MESH = pl.DeviceIdType.MESH
HEADS, DH, TOK, GROUP = 16, 128, 128, 32
WIDTH = HEADS * DH
CHUNKS = 8
CW = WIDTH // CHUNKS
HPC = HEADS // CHUNKS
AHEAD = 3
LATE = 2
NEG = -1e30
F32 = jnp.float32
BF16 = jnp.bfloat16


def nt(a, b):
    return lax.dot_general(a, b, (((1,), (1,)), ((), ())), preferred_element_type=F32)


def nn(a, b):
    return lax.dot_general(a, b, (((1,), (0,)), ((), ())), preferred_element_type=F32)


def kernel(
    order, q_in, k_in, v_in, g_in, w_in, o_in, l_in,
    dqb, dkb, dvb,
    qb, kb, vb, gb, ob, ab, wx, po, ps, pr, lb, db, bias_s, bias_t,
    local_sem, w_send, w_recv, f_send, f_recv, p_send, p_recv,
    a_send, a_recv, kv_send, kv_recv, q_send, q_recv, s_send, s_recv, g_send, g_recv, ready,
):
    dp = lax.axis_index("dp")
    ctx = lax.axis_index("ctx")
    x, yh, core = dp // 4, (dp // 2) % 2, dp % 2
    yl, z = ctx // 16, ctx % 16

    def chip(x, yh, core):
        return x * 4 + yh * 2 + core

    right = (chip((x + 1) % 4, yh, core), ctx)
    left = (chip((x + 3) % 4, yh, core), ctx)
    across = (chip(x, 1 - yh, core), (1 - yl) * 16 + z)
    partner = (chip(x, yh, 1 - core), ctx)
    after = (dp, (ctx + 1) % 32)
    before = (dp, (ctx + 31) % 32)

    def cols(j):
        return pl.ds(pl.multiple_of(j * CW, CW), CW)

    def remote(src, dst, send, recv, device):
        return pltpu.make_async_remote_copy(
            src_ref=src, dst_ref=dst, send_sem=send, recv_sem=recv,
            device_id=device, device_id_type=MESH,
        )

    loads = [
        pltpu.make_async_copy(w_in, wx.at[0, core], local_sem.at[0]),
        pltpu.make_async_copy(q_in.at[0], qb.at[0], local_sem.at[1]),
        pltpu.make_async_copy(k_in.at[0], kb.at[0], local_sem.at[2]),
        pltpu.make_async_copy(v_in.at[0], vb.at[0], local_sem.at[3]),
        pltpu.make_async_copy(o_in.at[0], ob, local_sem.at[4]),
        pltpu.make_async_copy(l_in.at[0], lb.at[0], local_sem.at[5]),
    ]

    def strip(r, of_class):
        return pl.ds(pl.multiple_of(((x + r) % 4) * 512 + of_class * 256, 256), 256)

    for r in range(4):
        loads.append(
            pltpu.make_async_copy(
                g_in.at[0, :, strip(r, yh)],
                ab.at[pl.ds(0, TOK), pl.ds(r * 256, 256)],
                local_sem.at[6 + r],
            )
        )
    for c in loads:
        c.start()

    barrier = pltpu.get_barrier_semaphore()
    up_waits, down_waits = z == 15, z != 0

    def tell(semaphore, device):
        pl.semaphore_signal(semaphore, inc=1, device_id=device, device_id_type=MESH)

    for device in (right, left, across, partner):
        tell(barrier, device)
    pl.when(z != 15)(lambda: tell(barrier, after))
    pl.when(z == 0)(lambda: tell(barrier, before))
    pl.semaphore_wait(barrier, 4 + up_waits.astype(jnp.int32) + down_waits.astype(jnp.int32))

    def own_right(j):
        return remote(w_in.at[:, cols(j)], wx.at[3, core, :, cols(j)], w_send.at[0, j], w_recv.at[0, j], right)

    def own_left(j):
        return remote(w_in.at[:, cols(j)], wx.at[1, core, :, cols(j)], w_send.at[1, j], w_recv.at[1, j], left)

    low, high = pl.ds(0, TOK // 2), pl.ds(TOK // 2, TOK // 2)

    def far_right(j):
        return remote(
            wx.at[3, core, low, cols(j)], wx.at[2, core, low, cols(j)], f_send.at[0, j], f_recv.at[0, j], right
        )

    def far_left(j):
        return remote(
            wx.at[1, core, high, cols(j)], wx.at[2, core, high, cols(j)], f_send.at[1, j], f_recv.at[1, j], left
        )

    def share(r, j, owner):
        src = w_in.at[:, cols(j)] if r == 0 else wx.at[r, owner, :, cols(j)]
        return remote(src, wx.at[r, owner, :, cols(j)], p_send.at[r, j], p_recv.at[r, j], partner)

    def columns_across(r):
        return remote(
            g_in.at[0, :, strip(r, 1 - yh)],
            ab.at[pl.ds(TOK, TOK), pl.ds(r * 256, 256)],
            a_send.at[r], a_recv.at[r], across,
        )

    def key_after(j):
        return remote(k_in.at[0, :, cols(j)], kb.at[1, :, cols(j)], kv_send.at[0, j], kv_recv.at[0, j], after)

    def value_after(j):
        return remote(v_in.at[0, :, cols(j)], vb.at[1, :, cols(j)], kv_send.at[1, j], kv_recv.at[1, j], after)

    def query_before(j):
        return remote(q_in.at[0, :, cols(j)], qb.at[1, :, cols(j)], q_send.at[j], q_recv.at[j], before)

    lse_before = remote(l_in.at[0], lb.at[1], q_send.at[CHUNKS], q_recv.at[CHUNKS], before)

    def partial_across(j):
        return remote(ps.at[:, cols(j)], pr.at[:, cols(j)], s_send.at[j], s_recv.at[j], across)

    def grad_before(j):
        return remote(gb.at[0, :, cols(j)], gb.at[1, :, cols(j)], g_send.at[0, j], g_recv.at[0, j], before)

    def delta_before(j):
        return remote(db.at[0, j], db.at[1, j], g_send.at[1, j], g_recv.at[1, j], before)

    for j in range(AHEAD):
        own_right(j).start()
        own_left(j).start()
        if j == 0:
            for r in range(4):
                columns_across(r).start()
    pl.when(z == 15)(lambda: tell(ready.at[1], after))
    pl.when(z != 0)(lambda: tell(ready.at[0], before))

    @pl.loop(0, CHUNKS)
    def _(j):
        share(0, j, core).start()

    def send_down():
        pl.when(z == 0)(lambda: pl.semaphore_wait(ready.at[1], 1))
        lse_before.start()

        @pl.loop(0, CHUNKS)
        def _(j):
            query_before(j).start()

    def send_up():
        pl.when(z != 15)(lambda: pl.semaphore_wait(ready.at[0], 1))

        @pl.loop(0, CHUNKS)
        def _(j):
            key_after(j).start()
            value_after(j).start()

    pl.when(z != 0)(send_down)
    pl.when(z != 1)(send_up)

    sub = lax.broadcasted_iota(jnp.int32, (TOK, TOK), 0)
    lane = lax.broadcasted_iota(jnp.int32, (TOK, TOK), 1)

    def position(block, index):
        ids = [order[0, block * 4 + i] for i in range(4)]
        group = index // GROUP
        return jnp.where(group == 0, ids[0], jnp.where(group == 1, ids[1], jnp.where(group == 2, ids[2], ids[3]))) * GROUP + index % GROUP

    own_col, own_row = position(ctx, sub), position(ctx, lane)
    prev_row = position((ctx + 31) % 32, lane)
    next_row = position((ctx + 1) % 32, lane)
    zero = jnp.zeros((TOK, TOK), F32)
    neg = jnp.full((TOK, TOK), NEG, F32)
    bias_s[:, pl.ds(0, TOK)] = jnp.where(own_row <= own_col, zero, neg)
    bias_s[:, pl.ds(TOK, TOK)] = jnp.where(prev_row <= own_col, zero, neg)
    bias_t[:, pl.ds(0, TOK)] = jnp.where(own_col <= own_row, zero, neg)
    bias_t[:, pl.ds(TOK, TOK)] = jnp.where(own_col <= next_row, zero, neg)

    factor = DH ** -0.5

    def head_cols(j, h):
        return pl.ds(pl.multiple_of(j * CW + h * DH, DH), DH)

    def relay(j):
        own_right(j).wait_recv()
        far_right(j).start()
        share(3, j, core).start()
        own_left(j).wait_recv()
        far_left(j).start()
        share(1, j, core).start()

        @pl.when(j + AHEAD < CHUNKS)
        def _():
            own_right(j + AHEAD).start()
            own_left(j + AHEAD).start()

    def relay_far(j):
        far_right(j).wait_recv()
        far_left(j).wait_recv()
        share(2, j, core).start()

    def project(j):
        @pl.when(j == 0)
        def _():
            loads[0].wait()
            for r in range(4):
                loads[6 + r].wait()
                columns_across(r).wait_recv()

        for r in (0, 3, 1, 2):
            share(r, j, 1 - core).wait_recv()
        w = wx[:, :, :, cols(j)].reshape(8 * TOK, CW)
        part = nn(ab[...], w)
        ps[:, cols(j)] = part[TOK:].astype(BF16)
        partial_across(j).start()
        po[:, cols(j)] = part[:TOK]

    def queries_side(j):
        @pl.when(j == 0)
        def _():
            for c in loads[1:6]:
                c.wait()

        partial_across(j).wait_recv()
        grad = (po[:, cols(j)] + pr[:, cols(j)].astype(F32)).astype(BF16)
        gb[0, :, cols(j)] = grad
        grad_before(j).start()
        terms = grad.astype(F32) * ob[:, cols(j)].astype(F32)
        deltas = [jnp.sum(terms[:, h * DH:(h + 1) * DH], axis=1, keepdims=True) for h in range(HPC)]
        table = jnp.broadcast_to(deltas[0], (TOK, TOK))
        for h in range(1, HPC):
            table = jnp.where(lane == h, deltas[h], table)
        db[0, j] = table.T[:8]
        delta_before(j).start()
        key_after(j).wait_recv()
        value_after(j).wait_recv()
        for h in range(HPC):
            hc = head_cols(j, h)
            q, g = qb[0, :, hc], grad[:, h * DH:(h + 1) * DH]
            k = kb[:, :, hc].reshape(2 * TOK, DH)
            v = vb[:, :, hc].reshape(2 * TOK, DH)
            lse = jnp.broadcast_to(lb[0, pl.ds(j * HPC + h, 1)], (TOK, TOK)).T
            lse = jnp.concatenate([lse, lse], axis=1)
            p = jnp.exp(nt(q, k) * factor - lse + bias_s[...])
            ds = (p * (nt(g, v) - deltas[h])).astype(BF16)
            dqb[:, hc] = (nn(ds, k) * factor).astype(BF16)

    def keys_side(j):
        @pl.when(j == 0)
        def _():
            lse_before.wait_recv()

        query_before(j).wait_recv()
        grad_before(j).wait_recv()
        delta_before(j).wait_recv()
        for h in range(HPC):
            hc = head_cols(j, h)
            k, v = kb[0, :, hc], vb[0, :, hc]
            q = qb[:, :, hc].reshape(2 * TOK, DH)
            g = gb[:, :, hc].reshape(2 * TOK, DH)
            row = pl.ds(j * HPC + h, 1)
            lse = jnp.concatenate([lb[0, row], lb[1, row]], axis=1)
            delta = jnp.concatenate([db[0, j, pl.ds(h, 1)], db[1, j, pl.ds(h, 1)]], axis=1)
            p = jnp.exp(nt(k, q) * factor - lse + bias_t[...])
            dvb[:, hc] = nn(p.astype(BF16), g).astype(BF16)
            ds = (p * (nt(v, g) - delta)).astype(BF16)
            dkb[:, hc] = (nn(ds, q) * factor).astype(BF16)

    stages = ((relay, 0), (relay_far, 2), (project, 3), (queries_side, 5), (keys_side, 7))

    @pl.loop(0, CHUNKS + stages[-1][1])
    def _(t):
        for stage, lag in stages:
            pl.when((t >= lag) & (t < CHUNKS + lag))(functools.partial(stage, t - lag))
        pl.when((t == LATE) & (z == 0))(send_down)
        pl.when((t == LATE) & (z == 1))(send_up)

    for r in range(4):
        columns_across(r).wait_send()
    lse_before.wait_send()

    @pl.loop(0, CHUNKS)
    def _(j):
        for c in (own_right, own_left, far_right, far_left, key_after, value_after, query_before, partial_across,
                  grad_before, delta_before):
            c(j).wait_send()
        for r in range(4):
            share(r, j, core).wait_send()


def store(a, b, c, x, y, z, sem):
    copies = [pltpu.make_async_copy(s, d.at[0], sem.at[i]) for i, (s, d) in enumerate(((a, x), (b, y), (c, z)))]
    for copy in copies:
        copy.start()
    for copy in copies:
        copy.wait()


def on_device(queries, keys, values, out_grad, out_proj, attn_out, log_sum, group_order):
    hbm = pl.BlockSpec(memory_space=pl.ANY)
    vmem = pl.BlockSpec(memory_space=pltpu.VMEM)
    out = jax.ShapeDtypeStruct((1, TOK, WIDTH), BF16)
    dma = pltpu.SemaphoreType.DMA
    held = pl.pallas_call(
        kernel,
        out_shape=(pltpu.VMEM((TOK, WIDTH), BF16),) * 3,
        in_specs=[pl.BlockSpec(memory_space=pltpu.SMEM)] + [hbm] * 7,
        out_specs=(vmem, vmem, vmem),
        scratch_shapes=[
            pltpu.VMEM((2, TOK, WIDTH), BF16),
            pltpu.VMEM((2, TOK, WIDTH), BF16),
            pltpu.VMEM((2, TOK, WIDTH), BF16),
            pltpu.VMEM((2, TOK, WIDTH), BF16),
            pltpu.VMEM((TOK, WIDTH), BF16),
            pltpu.VMEM((2 * TOK, 1024), BF16),
            pltpu.VMEM((4, 2, TOK, WIDTH), BF16),
            pltpu.VMEM((TOK, WIDTH), F32),
            pltpu.VMEM((TOK, WIDTH), BF16),
            pltpu.VMEM((TOK, WIDTH), BF16),
            pltpu.VMEM((2, HEADS, TOK), F32),
            pltpu.VMEM((2, CHUNKS, 8, TOK), F32),
            pltpu.VMEM((TOK, 2 * TOK), F32),
            pltpu.VMEM((TOK, 2 * TOK), F32),
            dma((10,)),
            dma((2, CHUNKS)), dma((2, CHUNKS)),
            dma((2, CHUNKS)), dma((2, CHUNKS)),
            dma((4, CHUNKS)), dma((4, CHUNKS)),
            dma((4,)), dma((4,)),
            dma((2, CHUNKS)), dma((2, CHUNKS)),
            dma((CHUNKS + 1,)), dma((CHUNKS + 1,)),
            dma((CHUNKS,)), dma((CHUNKS,)),
            dma((2, CHUNKS)), dma((2, CHUNKS)),
            pltpu.SemaphoreType.REGULAR((2,)),
        ],
        compiler_params=pltpu.CompilerParams(collective_id=0, has_side_effects=True),
        name="attention_backward",
    )(group_order, queries, keys, values, out_grad, out_proj, attn_out, log_sum)
    return pl.pallas_call(
        store,
        out_shape=(out, out, out),
        in_specs=[vmem] * 3,
        out_specs=(hbm, hbm, hbm),
        scratch_shapes=[dma((3,))],
        name="store",
    )(*(pltpu.with_memory_space_constraint(h, pltpu.VMEM) for h in held))


def solution(mesh):
    block = P("dp", "ctx", None)
    return jax.shard_map(
        on_device,
        mesh=mesh,
        in_specs=(block, block, block, block, P("dp", None), block, P("dp", None, "ctx"), P("dp", None)),
        out_specs=(block, block, block),
        check_vma=False,
    )
```

time: 188 us -> 44.5 us (0.24)
  waiting for transfers between devices: 106 us -> 0 us
  Pallas kernels: 0 us -> 43.7 us
  matrix products: 21.2 us -> 0 us
  local copies, waits for them, and re-layouts: 21 us -> 0 us
  starting transfers between devices: 16.6 us -> 0 us
  between operations: 14.2 us -> 0.64 us
  other arithmetic: 7.12 us -> 0 us
    all_gather x1 -> x0, waiting for transfers between devices: 57.5 us -> none  [on_device(): lax.all_gather(out_proj, 'dp', axis=0, tiled=True)]
    ppermute x4 -> x0, waiting for transfers between devices: 48.2 us -> none  [shifted(): lax.ppermute(array, axis, [(i, (i + by) % size) for i in range(size)])]
    pallas_call x0 -> x2, Pallas kernels: none -> 43.7 us  [the longest x1 42.5 us: on_device(): pl.pallas_call(kernel, out_shape=(pltpu.VMEM((TOK, WIDTH), BF16),) * 3, i...]
    dot_general x11 -> x0, matrix products: 21.2 us -> none  [the longest x1 4.65 us: on_device(): jnp.dot(upstream, lax.all_gather(out_proj, 'dp', axis=0, tiled=True), pre...]
    ppermute x4 -> x0, starting transfers between devices: 16.6 us -> none  [shifted(): lax.ppermute(array, axis, [(i, (i + by) % size) for i in range(size)])]
    unnamed x18 -> x0, local copies, waits for them, and re-layouts: 8.2 us -> none
    reshape x3 -> x0, local copies, waits for them, and re-layouts: 5.56 us -> none  [the longest x2 5.09 us: pair_grads(): value_part.reshape(key_blk.shape[0], width)]
    mul x2 -> x0, local copies, waits for them, and re-layouts: 4.11 us -> none  [pair_grads(): jnp.einsum('hqk,qhd->khd', dscores, query_blk, preferred_element_type=jnp...]
  transfers between devices with their start and end apart: 5 -> 0, of which waited for: 4 -> 0; matrix products, arithmetic and copies ran while one was open for 22% -> 0% of each run, Pallas kernels for 0% -> 0%
where the time goes in v1:
time: 44.5 us; the launch traced here: 44.3 us
  Pallas kernels  43.7 us (98%)
  between operations  0.64 us (1%)
    pallas_call x1, Pallas kernels, on_device(): pl.pallas_call(kernel, out_shape=(pltpu.VMEM((TOK, WIDTH), BF16),) * 3, i...  42.5 us
    pallas_call x1, Pallas kernels, on_device(): pl.pallas_call(store, out_shape=(out, out, out), in_specs=[vmem] * 3, out...  1.17 us

profile of v1, /device:TPU:1, one launch (start us, length us, event | category | flops | bytes accessed | tf_op | source)
XLA Modules:
  0.0 44.3 jit_solution(9921266085110643915)
XLA Ops:
  0.6 42.5 %attention_backward.1 = (bf16[128,2048]{1,0:T(8,128)(2,1)S(1)}, bf16[128,2048]{1,0:T(8,128)(2,1)S(1)}, bf16[128,2048]{1,0:T(8,128)(2,1)S(1)}) custom-call(s32[1,128]{1,0:T(1,128)} %order.1, bf16[1,128,2048]{2,1,0:T(8,128)(2,1)} %q_in.1, bf16[1,128,2048]{2,1,0:T(8,128)(2,1)} %k_in.1, bf16[1,128,2048]{2,1,0:T(8,128)(2,1)} %v_in.1, bf16[1,128,2048]{2,1,0:T(8,128)(2,1)} %g_in.1, ...), custom_call_target="tpu_custom_call" | custom-call | tf_op jit(solution)/shard_map/attention_backward/pallas_call | solution.py:321
  43.1 1.2 %store.1 = (bf16[1,128,2048]{2,1,0:T(8,128)(2,1)}, bf16[1,128,2048]{2,1,0:T(8,128)(2,1)}, bf16[1,128,2048]{2,1,0:T(8,128)(2,1)}) custom-call(bf16[128,2048]{1,0:T(8,128)(2,1)S(1)} %get-tuple-element.6.a, bf16[128,2048]{1,0:T(8,128)(2,1)S(1)} %get-tuple-element.7.b, bf16[128,2048]{1,0:T(8,128)(2,1)S(1)} %get-tuple-element.8.c), custom_call_target="tpu_custom_call" | custom-call | tf_op jit(solution)/shard_map/store/pallas_call | solution.py:355

commit v2 on v1

--- a/solution.py
+++ b/solution.py
@@ -15,6 +15,7 @@
 HPC = HEADS // CHUNKS
 AHEAD = 3
 LATE = 2
+WIDE = 1
 NEG = -1e30
 F32 = jnp.float32
 BF16 = jnp.bfloat16
@@ -53,6 +54,9 @@
     def cols(j):
         return pl.ds(pl.multiple_of(j * CW, CW), CW)
 
+    def wide(j):
+        return pl.ds(pl.multiple_of(j * WIDE * CW, WIDE * CW), WIDE * CW)
+
     def remote(src, dst, send, recv, device):
         return pltpu.make_async_remote_copy(
             src_ref=src, dst_ref=dst, send_sem=send, recv_sem=recv,
@@ -71,12 +75,12 @@
     def strip(r, of_class):
         return pl.ds(pl.multiple_of(((x + r) % 4) * 512 + of_class * 256, 256), 256)
 
-    for r in range(4):
+    for i, r in enumerate((0, 2, 1, 3)):
         loads.append(
             pltpu.make_async_copy(
                 g_in.at[0, :, strip(r, yh)],
-                ab.at[pl.ds(0, TOK), pl.ds(r * 256, 256)],
-                local_sem.at[6 + r],
+                ab.at[pl.ds(0, TOK), pl.ds(i * 256, 256)],
+                local_sem.at[6 + i],
             )
         )
     for c in loads:
@@ -98,39 +102,47 @@
         return remote(w_in.at[:, cols(j)], wx.at[3, core, :, cols(j)], w_send.at[0, j], w_recv.at[0, j], right)
 
     def own_left(j):
-        return remote(w_in.at[:, cols(j)], wx.at[1, core, :, cols(j)], w_send.at[1, j], w_recv.at[1, j], left)
+        return remote(w_in.at[:, cols(j)], wx.at[2, core, :, cols(j)], w_send.at[1, j], w_recv.at[1, j], left)
 
     low, high = pl.ds(0, TOK // 2), pl.ds(TOK // 2, TOK // 2)
 
     def far_right(j):
         return remote(
-            wx.at[3, core, low, cols(j)], wx.at[2, core, low, cols(j)], f_send.at[0, j], f_recv.at[0, j], right
+            wx.at[3, core, low, cols(j)], wx.at[1, core, low, cols(j)], f_send.at[0, j], f_recv.at[0, j], right
         )
 
     def far_left(j):
         return remote(
-            wx.at[1, core, high, cols(j)], wx.at[2, core, high, cols(j)], f_send.at[1, j], f_recv.at[1, j], left
-        )
-
-    def share(r, j, owner):
-        src = w_in.at[:, cols(j)] if r == 0 else wx.at[r, owner, :, cols(j)]
-        return remote(src, wx.at[r, owner, :, cols(j)], p_send.at[r, j], p_recv.at[r, j], partner)
-
-    def columns_across(r):
+            wx.at[2, core, high, cols(j)], wx.at[1, core, high, cols(j)], f_send.at[1, j], f_recv.at[1, j], left
+        )
+
+    def share_own(owner):
+        return remote(w_in, wx.at[0, owner], p_send.at[0, 0], p_recv.at[0, 0], partner)
+
+    def share_near(j, owner):
+        part = wx.at[pl.ds(2, 2), owner, :, cols(j)]
+        return remote(part, part, p_send.at[1, j], p_recv.at[1, j], partner)
+
+    def share_far(j, owner):
+        part = wx.at[1, owner, :, cols(j)]
+        return remote(part, part, p_send.at[2, j], p_recv.at[2, j], partner)
+
+    def columns_across(i):
+        r = (0, 2, 1, 3)[i]
         return remote(
             g_in.at[0, :, strip(r, 1 - yh)],
-            ab.at[pl.ds(TOK, TOK), pl.ds(r * 256, 256)],
-            a_send.at[r], a_recv.at[r], across,
+            ab.at[pl.ds(TOK, TOK), pl.ds(i * 256, 256)],
+            a_send.at[i], a_recv.at[i], across,
         )
 
     def key_after(j):
-        return remote(k_in.at[0, :, cols(j)], kb.at[1, :, cols(j)], kv_send.at[0, j], kv_recv.at[0, j], after)
+        return remote(k_in.at[0, :, wide(j)], kb.at[1, :, wide(j)], kv_send.at[0, j], kv_recv.at[0, j], after)
 
     def value_after(j):
-        return remote(v_in.at[0, :, cols(j)], vb.at[1, :, cols(j)], kv_send.at[1, j], kv_recv.at[1, j], after)
+        return remote(v_in.at[0, :, wide(j)], vb.at[1, :, wide(j)], kv_send.at[1, j], kv_recv.at[1, j], after)
 
     def query_before(j):
-        return remote(q_in.at[0, :, cols(j)], qb.at[1, :, cols(j)], q_send.at[j], q_recv.at[j], before)
+        return remote(q_in.at[0, :, wide(j)], qb.at[1, :, wide(j)], q_send.at[j], q_recv.at[j], before)
 
     lse_before = remote(l_in.at[0], lb.at[1], q_send.at[CHUNKS], q_recv.at[CHUNKS], before)
 
@@ -152,22 +164,20 @@
     pl.when(z == 15)(lambda: tell(ready.at[1], after))
     pl.when(z != 0)(lambda: tell(ready.at[0], before))
 
-    @pl.loop(0, CHUNKS)
-    def _(j):
-        share(0, j, core).start()
+    share_own(core).start()
 
     def send_down():
         pl.when(z == 0)(lambda: pl.semaphore_wait(ready.at[1], 1))
         lse_before.start()
 
-        @pl.loop(0, CHUNKS)
+        @pl.loop(0, CHUNKS // WIDE)
         def _(j):
             query_before(j).start()
 
     def send_up():
         pl.when(z != 15)(lambda: pl.semaphore_wait(ready.at[0], 1))
 
-        @pl.loop(0, CHUNKS)
+        @pl.loop(0, CHUNKS // WIDE)
         def _(j):
             key_after(j).start()
             value_after(j).start()
@@ -201,10 +211,9 @@
     def relay(j):
         own_right(j).wait_recv()
         far_right(j).start()
-        share(3, j, core).start()
         own_left(j).wait_recv()
         far_left(j).start()
-        share(1, j, core).start()
+        share_near(j, core).start()
 
         @pl.when(j + AHEAD < CHUNKS)
         def _():
@@ -214,18 +223,19 @@
     def relay_far(j):
         far_right(j).wait_recv()
         far_left(j).wait_recv()
-        share(2, j, core).start()
+        share_far(j, core).start()
 
     def project(j):
         @pl.when(j == 0)
         def _():
             loads[0].wait()
+            share_own(1 - core).wait_recv()
             for r in range(4):
                 loads[6 + r].wait()
                 columns_across(r).wait_recv()
 
-        for r in (0, 3, 1, 2):
-            share(r, j, 1 - core).wait_recv()
+        share_near(j, 1 - core).wait_recv()
+        share_far(j, 1 - core).wait_recv()
         w = wx[:, :, :, cols(j)].reshape(8 * TOK, CW)
         part = nn(ab[...], w)
         ps[:, cols(j)] = part[TOK:].astype(BF16)
@@ -249,8 +259,11 @@
             table = jnp.where(lane == h, deltas[h], table)
         db[0, j] = table.T[:8]
         delta_before(j).start()
-        key_after(j).wait_recv()
-        value_after(j).wait_recv()
+        @pl.when(j % WIDE == 0)
+        def _():
+            key_after(j // WIDE).wait_recv()
+            value_after(j // WIDE).wait_recv()
+
         for h in range(HPC):
             hc = head_cols(j, h)
             q, g = qb[0, :, hc], grad[:, h * DH:(h + 1) * DH]
@@ -267,7 +280,10 @@
         def _():
             lse_before.wait_recv()
 
-        query_before(j).wait_recv()
+        @pl.when(j % WIDE == 0)
+        def _():
+            query_before(j // WIDE).wait_recv()
+
         grad_before(j).wait_recv()
         delta_before(j).wait_recv()
         for h in range(HPC):
@@ -295,14 +311,20 @@
     for r in range(4):
         columns_across(r).wait_send()
     lse_before.wait_send()
+    share_own(core).wait_send()
+
+    @pl.loop(0, CHUNKS // WIDE)
+    def _(j):
+        for c in (key_after, value_after, query_before):
+            c(j).wait_send()
 
     @pl.loop(0, CHUNKS)
     def _(j):
-        for c in (own_right, own_left, far_right, far_left, key_after, value_after, query_before, partial_across,
+        for c in (own_right, own_left, far_right, far_left, partial_across,
                   grad_before, delta_before):
             c(j).wait_send()
-        for r in range(4):
-            share(r, j, core).wait_send()
+        share_near(j, core).wait_send()
+        share_far(j, core).wait_send()
 
 
 def store(a, b, c, x, y, z, sem):
@@ -341,7 +363,7 @@
             dma((10,)),
             dma((2, CHUNKS)), dma((2, CHUNKS)),
             dma((2, CHUNKS)), dma((2, CHUNKS)),
-            dma((4, CHUNKS)), dma((4, CHUNKS)),
+            dma((3, CHUNKS)), dma((3, CHUNKS)),
             dma((4,)), dma((4,)),
             dma((2, CHUNKS)), dma((2, CHUNKS)),
             dma((CHUNKS + 1,)), dma((CHUNKS + 1,)),

time: 44.5 us -> 44.4 us (level)
  no operation moved by 1% of the time
where the time goes in v2:
time: 44.4 us; the launch traced here: 44.1 us
  Pallas kernels  43.4 us (98%)
  between operations  0.64 us (1%)
    pallas_call x1, Pallas kernels, on_device(): pl.pallas_call(kernel, out_shape=(pltpu.VMEM((TOK, WIDTH), BF16),) * 3, i...  42.3 us
    pallas_call x1, Pallas kernels, on_device(): pl.pallas_call(store, out_shape=(out, out, out), in_specs=[vmem] * 3, out...  1.17 us

profile of v2, /device:TPU:1, one launch (start us, length us, event | category | flops | bytes accessed | tf_op | source)
XLA Modules:
  0.0 44.1 jit_solution(12321055749910444444)
XLA Ops:
  0.6 42.3 %attention_backward.1 = (bf16[128,2048]{1,0:T(8,128)(2,1)S(1)}, bf16[128,2048]{1,0:T(8,128)(2,1)S(1)}, bf16[128,2048]{1,0:T(8,128)(2,1)S(1)}) custom-call(s32[1,128]{1,0:T(1,128)} %order.1, bf16[1,128,2048]{2,1,0:T(8,128)(2,1)} %q_in.1, bf16[1,128,2048]{2,1,0:T(8,128)(2,1)} %k_in.1, bf16[1,128,2048]{2,1,0:T(8,128)(2,1)} %v_in.1, bf16[1,128,2048]{2,1,0:T(8,128)(2,1)} %g_in.1, ...), custom_call_target="tpu_custom_call" | custom-call | tf_op jit(solution)/shard_map/attention_backward/pallas_call | solution.py:343
  42.9 1.2 %store.1 = (bf16[1,128,2048]{2,1,0:T(8,128)(2,1)}, bf16[1,128,2048]{2,1,0:T(8,128)(2,1)}, bf16[1,128,2048]{2,1,0:T(8,128)(2,1)}) custom-call(bf16[128,2048]{1,0:T(8,128)(2,1)S(1)} %get-tuple-element.6.a, bf16[128,2048]{1,0:T(8,128)(2,1)S(1)} %get-tuple-element.7.b, bf16[128,2048]{1,0:T(8,128)(2,1)S(1)} %get-tuple-element.8.c), custom_call_target="tpu_custom_call" | custom-call | tf_op jit(solution)/shard_map/store/pallas_call | solution.py:377
